TPU v7x, 512 devices: a whole 4x8x8 slice. The times are simulated.
512 devices in a mesh: slab: 64 (over x, y, z_lo), grp: 8 (over z_hi, core).
Axes of the slice: x: 4, y: 8, z: 8 (z_hi: 4, z_lo: 2; z = z_hi * 2 + z_lo), core: 2. Of those that a mesh axis runs over, the one named last changes fastest.
Arguments:
- echo_data: bfloat16 [64, 1024, 2048], P('slab', 'grp'), may hold values from -6 to 6
- acquirer: int32 [3], replicated, may hold values from 0 to 63, as said below
- panels: bfloat16 [64, 3, 64, 128, 128], P('slab', None, 'grp'), may hold values from -0.00390625 to 0.00390625
- block_count: int32 [64, 3], P('slab'), may hold values from 16 to 64, as said below
- block_rows: int32 [64, 3, 64], P('slab'), may hold values from 0 to 7
- block_columns: int32 [64, 3, 64], P('slab'), may hold values from 0 to 15
- apodization: float32 [16, 1024], P(None, 'grp'), may hold values from 0.25 to 2.5
- window_index: int32 [65536], P('slab'), may hold values from 0 to 15
Outputs:
- image: float32 [65536], P(('slab', 'grp'))
Inputs may be any that keep to these rules, and one draw needn't show every extreme that they name: `acquirer`: 3 distinct slab indices, the last slab index always among them. `block_count`: slots below the count are live, the others unused; some slab and transmit has all 64 live in every draw.
All inputs are finite; a program needn't handle non-finite values.
Results may differ from a plain program's by a relative error of at most 0.0003.
Values may be sent and summed in bfloat16 or wider, within the bound.
No kernel may reach another device: no remote copies, remote signals or barrier semaphores. Data moves between devices by JAX's collectives and lax.ppermute only.
A program may use at most 128 MiB of HBM per device.

v0:
```python
import math
import jax
import jax.numpy as jnp
from jax import lax
from jax.sharding import PartitionSpec as P


def from_root(block, axis, holder):
    block = jnp.where(lax.axis_index(axis) == holder, block, jnp.zeros_like(block))
    return lax.psum(block, axis)


def table_rows(window_index, table):
    windows = table.shape[0]
    onehot = (window_index[:, None] == jnp.arange(windows, dtype=jnp.int32)[None, :]).astype(
        jnp.float32
    )
    return jnp.dot(
        onehot, table, precision=lax.Precision.HIGHEST, preferred_element_type=jnp.float32
    )


def block_terms(piece, columns, signal):
    block_size = piece.shape[-1]
    channels = signal.shape[0]
    grid = signal.reshape(channels, signal.shape[1] // block_size, block_size)
    picked = jnp.take(grid, columns, axis=1)
    return jnp.einsum("kvs,cks->kvc", piece, picked, preferred_element_type=jnp.float32)


def place_rows(terms, rows, live, row_blocks):
    onehot = (rows[:, None] == jnp.arange(row_blocks, dtype=jnp.int32)[None, :]).astype(
        jnp.float32
    ) * live[:, None]
    return jnp.einsum("kr,kvc->rvc", onehot, terms, precision=lax.Precision.HIGHEST)


def masked_slots(running, piece, rows, columns, live, signal):
    width = piece.shape[0]
    block_size = piece.shape[-1]
    channels = signal.shape[0]
    limit = max(1, (1 << 18) // (block_size * channels))
    group = math.gcd(width, limit)
    turns = width // group
    grouped = (
        piece.reshape(turns, group, block_size, block_size),
        rows.reshape(turns, group),
        columns.reshape(turns, group),
        live.reshape(turns, group),
    )

    def one_group(current, inputs):
        group_piece, group_rows, group_columns, group_live = inputs
        terms = block_terms(group_piece, group_columns, signal)
        return (current + place_rows(terms, group_rows, group_live, current.shape[0]), None)

    result, unused = lax.scan(one_group, running, grouped)
    return result


def add_slots(running, piece, rows_all, columns_all, count, signal):
    width = piece.shape[0]
    live = (jnp.arange(width, dtype=jnp.int32) < count).astype(jnp.float32)
    return masked_slots(running, piece, rows_all, columns_all, live, signal)


def per_device(
    echo_data, acquirer, panels, block_count, block_rows, block_columns, apodization, window_index
):
    signal_own = echo_data[0]
    block_size = panels.shape[-1]
    voxel_count = window_index.shape[0]
    row_blocks = voxel_count // block_size
    weights = table_rows(window_index, apodization)
    running = jnp.zeros((row_blocks, block_size, signal_own.shape[0]), jnp.float32)
    for transmit in range(acquirer.shape[0]):
        signal = from_root(signal_own, "slab", acquirer[transmit])
        rows_all = block_rows[0, transmit]
        columns_all = block_columns[0, transmit]
        count = block_count[0, transmit]

        def fold_panels(
            current,
            piece,
            start,
            signal=signal,
            rows_all=rows_all,
            columns_all=columns_all,
            count=count,
        ):
            return add_slots(current, piece, rows_all, columns_all, count, signal)

        running = fold_panels(
            running, lax.all_gather(panels[0, transmit], "grp", axis=0, tiled=True), jnp.int32(0)
        )
    partial_value = jnp.sum(running.reshape(voxel_count, running.shape[2]) * weights, axis=1)
    return lax.psum_scatter(partial_value, "grp", scatter_dimension=0, tiled=True)


def solution(mesh):
    return jax.shard_map(
        per_device,
        mesh=mesh,
        in_specs=(
            P("slab", "grp", None),
            P(),
            P("slab", None, "grp", None, None),
            P("slab", None),
            P("slab", None, None),
            P("slab", None, None),
            P(None, "grp"),
            P("slab"),
        ),
        out_specs=P(("slab", "grp")),
        check_vma=False,
    )
```

profile of v0, /device:TPU:1, one launch (start us, length us, event | category | flops | bytes accessed | tf_op | source)
XLA Modules:
  0.0 722.1 jit_solution(10459350146008842801)
XLA Ops:
  7.4 1.4 fusion.66
  20.4 580.0 %all-reduce.4.cloned.1.call-done = (bf16[128,2048]{0,1:T(8,128)(2,1)}, bf16[128,2048]{0,1:T(8,128)(2,1)}, bf16[128,2048]{0,1:T(8,128)(2,1)}) async-done(((bf16[128,2048]{0,1:T(8,128)(2,1)}, bf16[128,2048]{0,1:T(8,128)(2,1)}, bf16[128,2048]{0,1:T(8,128)(2,1)}), (bf16[128,2048]{0,1:T(8,128)(2,1)}, bf16[128,2048]{0,1:T(8,128)(2,1)}, bf16[128,2048]{0,1:T(8,128)(2,1)})) %all-reduce.4.cloned.1.call-update) | async-done | bytes 1572880 | tf_op jit(solution)/shard_map/psum | solution.py:10
  600.5 20.0 %while.33 = (s32[]{:T(128)}, f32[8,128,128]{2,0,1:T(8,128)S(1)}, s32[4,16]{1,0:T(4,128)S(1)}, f32[4,16]{1,0:T(4,128)S(1)}, bf16[4,16,128,128]{3,2,1,0:T(8,128)(2...) while((s32[]{:T(128)}, f32[8,128,128]{2,0,1:T(8,128)S(1)}, ...), condition=%wide.region_2.4_spmd.clone, body=%wide.region_1.3_spmd.clone.sunk | while | flops 92800352 | bytes 6296851 | solution.py:57
  600.5 1.4 copy.56
  602.5 1.6 fusion.107
  607.5 1.6 fusion.107
  612.5 1.6 fusion.107
  617.5 1.6 fusion.107
  620.5 15.9 %while.31 = (s32[]{:T(128)}, f32[8,128,128]{2,0,1:T(8,128)S(1)}, s32[4,16]{1,0:T(4,128)S(1)}, f32[4,16]{1,0:T(4,128)S(1)}, bf16[4,16,128,128]{3,2,1,0:T(8,128)(2...) while((s32[]{:T(128)}, f32[8,128,128]{2,0,1:T(8,128)S(1)}, s32[4,16]{1,0:T(4,128)S(1)}, ...), condition=%wide.region_5.7_spmd, body=%wide.region_4.6_spmd.sunk | while | flops 92669280 | bytes 6296833 | solution.py:57
  621.5 1.6 fusion.93
  623.2 1.3 convolution_add_fusion.6
  625.5 1.6 fusion.93
  627.2 1.3 convolution_add_fusion.6
  629.5 1.6 fusion.93
  631.1 1.3 convolution_add_fusion.6
  633.5 1.6 fusion.93
  636.5 15.9 %while.32 = (s32[]{:T(128)}, f32[8,128,128]{2,0,1:T(8,128)S(1)}, s32[4,16]{1,0:T(4,128)S(1)}, f32[4,16]{1,0:T(4,128)S(1)}, bf16[4,16,128,128]{3,2,1,0:T(8,128)(2...) while((s32[]{:T(128)}, f32[8,128,128]{2,0,1:T(8,128)S(1)}, ...), condition=%wide.region_8.10_spmd, body=%wide.region_7.9_spmd.sunk | while | flops 92669280 | bytes 6296833 | solution.py:57
  637.5 1.6 fusion.100
  641.5 1.6 fusion.100
  643.2 1.3 convolution_add_fusion.7
  645.5 1.6 fusion.100
  649.5 1.6 fusion.100
  651.1 1.3 convolution_add_fusion.7
  653.4 60.5 %all-reduce = f32[1024]{0:T(1024)S(1)} all-reduce(f32[1024]{0:T(1024)S(1)} %fusion.57), channel_id=5, replica_groups=mesh['slab'=64,'grp'=8] {'grp'}, use_global_device_ids=true, to_apply=%region_10.12.clone | all-reduce | flops 1024 | bytes 8192
  (124 shorter events, 34.4 us)
Async XLA Ops:
  7.4 645.4 %copy-start = (f32[16,128]{1,0:T(8,128)S(1)}, f32[16,128]{1,0:T(8,128)}, u32[]{:S(2)}) copy-start(f32[16,128]{1,0:T(8,128)} %param.22) | copy-start | bytes 24580
  7.4 593.1 %all-reduce.4.cloned.1.call-start = ((), (), s32[]{:S(2)}) async-start(), calls=%async_computation.3 | async-start | bytes 3145728 | tf_op jit(solution)/shard_map/psum | solution.py:10
  12.0 1.6 copy-start.3
  13.2 2.4 copy-start.6
  13.2 2.4 copy-start.7
  13.2 2.6 copy-start.4
  13.2 587.2 %all-gather.7.cloned.1.call-start = ((), (), s32[]{:S(2)}) async-start(), calls=%async_computation | async-start | bytes 2359296 | tf_op jit(solution)/shard_map/all_gather | solution.py:94
  14.4 606.1 %all-gather.9.cloned.1.call-start = ((), (), s32[]{:S(2)}) async-start(), calls=%async_computation.1 | async-start | bytes 2359296 | tf_op jit(solution)/shard_map/all_gather | solution.py:94
  15.0 621.5 %all-gather.11.cloned.1.call-start = ((), (), s32[]{:S(2)}) async-start(), calls=%async_computation.2 | async-start | bytes 2359296 | tf_op jit(solution)/shard_map/all_gather | solution.py:94
  600.5 20.0 %copy-start.2 = (bf16[128,2048]{0,1:T(8,128)(2,1)S(1)}, bf16[128,2048]{0,1:T(8,128)(2,1)}, u32[]{:S(2)}) copy-start(bf16[128,2048]{0,1:T(8,128)(2,1)} %get-tuple-element.389) | copy-start | bytes 1572868
  620.5 16.0 %copy-start.1 = (bf16[128,2048]{0,1:T(8,128)(2,1)S(1)}, bf16[128,2048]{0,1:T(8,128)(2,1)}, u32[]{:S(2)}) copy-start(bf16[128,2048]{0,1:T(8,128)(2,1)} %get-tuple-element.413) | copy-start | bytes 1572868
  636.5 16.3 %copy-start.5 = (s32[1024]{0:T(1024)S(1)}, s32[1024]{0:T(1024)}, u32[]{:S(2)}) copy-start(s32[1024]{0:T(1024)} %param.23) | copy-start | bytes 12292
Sparse Core Ops, SparseCore 0:
  13.4 587.0 all-reduce.3
Sparse Core Ops, SparseCore 1:
  15.9 46.7 all-gather.6
  64.8 39.5 all-gather.8
  106.6 39.3 all-gather.10
where the time goes:
time: 723 us; the launch traced here: 722 us
  waiting for transfers between devices  581 us (80%)
  blocking collectives  60.5 us (8%)
  matrix products  35.8 us (5%)
  local copies, waits for them, and re-layouts  22.7 us (3%)
  between operations  17.7 us (2%)
    psum x1, waiting for transfers between devices, from_root(): return lax.psum(block, axis)  580 us
    unnamed x1, blocking collectives  60.5 us
    dot_general x12, matrix products, block_terms(): jnp.einsum('kvs,cks->kvc', piece, picked, preferred_element_type=jnp.floa...  19.3 us
    dot_general x12, matrix products, place_rows(): jnp.einsum('kr,kvc->rvc', onehot, terms, precision=lax.Precision.HIGHEST)  15.9 us
  transfers between devices with their start and end apart: 4, of which 1 were waited for; matrix products, arithmetic and copies ran while one was open for 6% of the time, Pallas kernels for 0%

commit v1 on v0

--- a/solution.py
+++ b/solution.py
@@ -7,7 +7,7 @@
 
 def from_root(block, axis, holder):
     block = jnp.where(lax.axis_index(axis) == holder, block, jnp.zeros_like(block))
-    return lax.psum(block, axis)
+    return jnp.sum(lax.all_gather(block, axis), axis=0)
 
 
 def table_rows(window_index, table):

time: 723 us -> 2370 us (3.28)
  waiting for transfers between devices: 581 us -> 2240 us
  blocking collectives: 60.5 us -> 13.9 us
  other arithmetic: 3.25 us -> 38.3 us
    all_gather x0 -> x3, waiting for transfers between devices: none -> 2150 us  [from_root(): return jnp.sum(lax.all_gather(block, axis), axis=0)]
    psum x1 -> x0, waiting for transfers between devices: 580 us -> none  [from_root(): return lax.psum(block, axis)]
    all_gather x3, waiting for transfers between devices: 0.05 us -> 86.7 us  [per_device(): lax.all_gather(panels[0, transmit], 'grp', axis=0, tiled=True)]
    unnamed x1, blocking collectives: 60.5 us -> 13.9 us
    reduce_sum x0 -> x3, other arithmetic: none -> 34 us  [from_root(): return jnp.sum(lax.all_gather(block, axis), axis=0)]
  transfers between devices with their start and end apart: 4 -> 6, of which waited for: 1 -> 6; matrix products, arithmetic and copies ran while one was open for 6% -> 3% of each run, Pallas kernels for 0% -> 0%
where the time goes in v1:
time: 2370 us; the launch traced here: 2360 us
  waiting for transfers between devices  2240 us (95%)
  other arithmetic  38.3 us (2%)
  matrix products  35.9 us (2%)
    all_gather x3, waiting for transfers between devices, from_root(): return jnp.sum(lax.all_gather(block, axis), axis=0)  2150 us
    all_gather x3, waiting for transfers between devices, per_device(): lax.all_gather(panels[0, transmit], 'grp', axis=0, tiled=True)  86.7 us
  transfers between devices with their start and end apart: 6, of which 6 were waited for; matrix products, arithmetic and copies ran while one was open for 3% of the time, Pallas kernels for 0%

profile of v1, /device:TPU:1, one launch (start us, length us, event | category | flops | bytes accessed | tf_op | source)
XLA Modules:
  0.0 2364.7 jit_solution(10899181896365958502)
XLA Ops:
  9.8 2.2 broadcast_select_fusion
  20.4 724.3 %all-gather.10.cloned.1.call-done = bf16[64,128,2048]{2,1,0:T(8,128)(2,1)} async-done(((bf16[1,128,2048]{2,1,0:T(8,128)(2,1)}), bf16[64,128,2048]{2,1,0:T(8,128)(2,1)}) %all-gather.10.cloned.1.call-update) | async-done | bytes 33554448 | tf_op jit(solution)/shard_map/all_gather | solution.py:10
  744.7 11.3 reduce_sum.45
  756.3 31.6 %all-gather.16.cloned.1.call-done = bf16[1,1,64,128,128]{4,3,1,0,2:T(8,128)(2,1)} async-done(((bf16[1,1,8,128,128]{4,3,1,0,2:T(8,128)(2,1)}), bf16[1,1,64,128,128]{4,3,1,0,2:T(8,128)(2,1)}) %all-gather.16.cloned.1.call-update) | async-done | bytes 2097168 | tf_op jit(solution)/shard_map/all_gather | solution.py:94
  787.9 15.9 while.33
  788.9 1.6 fusion.107
  792.9 1.6 fusion.107
  796.9 1.6 fusion.107
  800.8 1.7 fusion.107
  803.9 710.4 %all-gather.12.cloned.1.call-done = bf16[64,128,2048]{2,1,0:T(8,128)(2,1)} async-done(((bf16[1,128,2048]{2,1,0:T(8,128)(2,1)}), bf16[64,128,2048]{2,1,0:T(8,128)(2,1)}) %all-gather.12.cloned.1.call-update) | async-done | bytes 33554448 | tf_op jit(solution)/shard_map/all_gather | solution.py:10
  1514.2 11.3 reduce_sum.46
  1525.9 718.0 %all-gather.14.cloned.1.call-done = bf16[64,128,2048]{2,1,0:T(8,128)(2,1)} async-done(((bf16[1,128,2048]{2,1,0:T(8,128)(2,1)}), bf16[64,128,2048]{2,1,0:T(8,128)(2,1)}) %all-gather.14.cloned.1.call-update) | async-done | bytes 33554448 | tf_op jit(solution)/shard_map/all_gather | solution.py:10
  2243.8 11.3 reduce_sum.47
  2255.5 31.4 %all-gather.18.cloned.1.call-done = bf16[1,1,64,128,128]{4,3,1,0,2:T(8,128)(2,1)} async-done(((bf16[1,1,8,128,128]{4,3,1,0,2:T(8,128)(2,1)}), bf16[1,1,64,128,128]{4,3,1,0,2:T(8,128)(2,1)}) %all-gather.18.cloned.1.call-update) | async-done | bytes 2097168 | tf_op jit(solution)/shard_map/all_gather | solution.py:94
  2286.9 15.9 while.31
  2291.9 1.6 fusion.93
  2295.9 1.6 fusion.93
  2299.9 1.6 fusion.93
  2302.9 23.7 %all-gather.20.cloned.1.call-done = bf16[1,1,64,128,128]{4,3,1,0,2:T(8,128)(2,1)} async-done(((bf16[1,1,8,128,128]{4,3,1,0,2:T(8,128)(2,1)}), bf16[1,1,64,128,128]{4,3,1,0,2:T(8,128)(2,1)}) %all-gather.20.cloned.1.call-update) | async-done | bytes 2097168 | tf_op jit(solution)/shard_map/all_gather | solution.py:94
  2326.6 15.9 while.32
  2327.5 1.6 fusion.100
  2331.5 1.6 fusion.100
  2339.5 1.6 fusion.100
  2343.4 13.9 all-reduce
  (131 shorter events, 42.3 us)
Async XLA Ops:
  6.5 2336.2 %copy-start = (f32[16,128]{1,0:T(8,128)S(1)}, f32[16,128]{1,0:T(8,128)}, u32[]{:S(2)}) copy-start(f32[16,128]{1,0:T(8,128)} %param.22) | copy-start | bytes 24580
  6.5 5.6 copy-start.1
  6.5 738.2 %all-gather.10.cloned.1.call-start = ((), (), s32[]{:S(2)}) async-start(), calls=%async_computation | async-start | bytes 34078720 | tf_op jit(solution)/shard_map/all_gather | solution.py:10
  12.0 3.6 copy-start.4
  12.0 3.6 copy-start.5
  12.0 3.8 copy-start.2
  12.1 775.8 %all-gather.16.cloned.1.call-start = ((), (), s32[]{:S(2)}) async-start(), calls=%async_computation.3 | async-start | bytes 2359296 | tf_op jit(solution)/shard_map/all_gather | solution.py:94
  13.1 1501.1 %all-gather.12.cloned.1.call-start = ((), (), s32[]{:S(2)}) async-start(), calls=%async_computation.1 | async-start | bytes 34078720 | tf_op jit(solution)/shard_map/all_gather | solution.py:10
  13.8 2230.0 %all-gather.14.cloned.1.call-start = ((), (), s32[]{:S(2)}) async-start(), calls=%async_computation.2 | async-start | bytes 34078720 | tf_op jit(solution)/shard_map/all_gather | solution.py:10
  14.4 2272.5 %all-gather.18.cloned.1.call-start = ((), (), s32[]{:S(2)}) async-start(), calls=%async_computation.4 | async-start | bytes 2359296 | tf_op jit(solution)/shard_map/all_gather | solution.py:94
  15.0 2311.6 %all-gather.20.cloned.1.call-start = ((), (), s32[]{:S(2)}) async-start(), calls=%async_computation.5 | async-start | bytes 2359296 | tf_op jit(solution)/shard_map/all_gather | solution.py:94
  2326.6 16.2 copy-start.3
Sparse Core Ops, SparseCore 0:
  12.2 732.4 all-gather.9
  746.9 41.0 all-gather.15
  790.0 724.1 all-gather.11
  1516.2 727.6 all-gather.13
  2245.8 41.0 all-gather.17
  2288.9 37.5 all-gather.19
